TPU v7x, 128 devices: a whole 4x4x4 slice. The times are simulated.
128 devices in a mesh: row: 8 (over z, y_hi), col: 16 (over y_lo, x, core).
Axes of the slice: x: 4, y: 4 (y_hi: 2, y_lo: 2; y = y_hi * 2 + y_lo), z: 4, core: 2. Of those that a mesh axis runs over, the one named last changes fastest.
Arguments:
- object_field: float32 [2, 2, 2048, 4096], P(None, None, 'row', 'col'), may hold values from -0.6 to 1
- probe_modes: float32 [2, 2, 256, 256], replicated, may hold values from -5 to 5
- amplitudes: float32 [2, 24, 16, 256, 256], P(None, 'row', 'col'), may hold values from 0 to 2
- offsets: int32 [2, 2, 24, 16], P(None, None, 'row', 'col'), may hold values from 0 to 255
- counts: int32 [2, 8, 16], P(None, 'row', 'col'), may hold values from 1 to 3, as said below
Outputs:
- new_object: float32 [2, 2, 2048, 4096], P(None, None, 'row', 'col')
- new_probe: float32 [2, 2, 256, 256], replicated
Inputs may be any that keep to these rules, and one draw needn't show every extreme that they name: offsets[b, 0, r * 3 + s, c] and offsets[b, 1, r * 3 + s, c] are the row and column, counted from tile (r, c)'s first cell, of the centre of slot s's 256 x 256 patch in batch b. Tile (r, c) has counts[b, r, c] scan positions in batch b, in its first slots; the other slots are unused; in each batch some tile has 3.
All inputs are finite; a program needn't handle non-finite values.
Results may differ from a plain program's by a relative error of at most 0.02.
Values sent between devices are 32-bit elements; how exact they have to be, the bound alone decides.
A program may use at most 128 MiB of HBM per device.

v0:
```python
import math
import jax
import jax.numpy as jnp
from jax import lax
from jax.sharding import PartitionSpec as P

AMPLITUDE_FLOOR = 0.5
OBJECT_STEP = 0.25
PROBE_STEP = 0.125


def from_behind(value, axis, steps):
    count = lax.axis_size(axis)
    leading, last = (max(0, -steps), min(count, count - steps))
    return lax.ppermute(value, axis, [(source, source + steps) for source in range(leading, last)])


def with_halo(array, sides, width):
    for axis, dim in sides:
        count, length = (lax.axis_size(axis), array.shape[dim])
        up = [(i, (i + 1) % count) for i in range(count - 1)]
        down = [(j, i) for i, j in up]
        last = lax.slice_in_dim(array, length - width, length, axis=dim)
        leading = lax.slice_in_dim(array, 0, width, axis=dim)
        before = lax.ppermute(last, axis, up)
        after = lax.ppermute(leading, axis, down)
        array = jnp.concatenate([before, array, after], axis=dim)
    return array


def tables(pattern_side):
    indices = jnp.arange(pattern_side, dtype=jnp.int32)
    products = indices[:, None] * indices[None, :] % pattern_side
    angles = products.astype(jnp.float32) * (2.0 * math.pi / pattern_side)
    norm_scale = 1.0 / math.sqrt(pattern_side)
    forward_re = (jnp.cos(angles) * norm_scale).astype(jnp.bfloat16)
    forward_im = (-jnp.sin(angles) * norm_scale).astype(jnp.bfloat16)
    frequency = jnp.where(indices < pattern_side // 2, indices, indices - pattern_side)
    phases = (frequency[:, None] * frequency[:, None] + frequency[None, :] * frequency[None, :]) % (
        16 * pattern_side
    )
    chirp_angles = phases.astype(jnp.float32) * (2.0 * math.pi / (16 * pattern_side))
    return (forward_re, forward_im, jnp.cos(chirp_angles), -jnp.sin(chirp_angles))


def contract(form, left, right):
    return jnp.einsum(form, left, right, preferred_element_type=jnp.float32)


def transform(field_re, field_im, table_re, table_im, inverse):
    sign_value = -1.0 if inverse else 1.0
    left_re = field_re.astype(jnp.bfloat16)
    left_im = field_im.astype(jnp.bfloat16)
    first_rr = contract("mjk,kl->mjl", left_re, table_re)
    first_ri = contract("mjk,kl->mjl", left_re, table_im)
    first_ir = contract("mjk,kl->mjl", left_im, table_re)
    first_ii = contract("mjk,kl->mjl", left_im, table_im)
    middle_re = (first_rr - sign_value * first_ii).astype(jnp.bfloat16)
    middle_im = (first_ir + sign_value * first_ri).astype(jnp.bfloat16)
    out_re = contract("jk,mkl->mjl", table_re, middle_re) - sign_value * contract(
        "jk,mkl->mjl", table_im, middle_im
    )
    out_im = contract("jk,mkl->mjl", table_re, middle_im) + sign_value * contract(
        "jk,mkl->mjl", table_im, middle_re
    )
    return (out_re, out_im)


def position_terms(patch_cells, probe_modes, amplitude, dft_table):
    forward_re, forward_im, chirp_re, chirp_im = dft_table
    slice_count = patch_cells.shape[1]
    wave_re = probe_modes[0]
    wave_im = probe_modes[1]
    incoming = []
    for slice_index in range(slice_count):
        incoming.append((wave_re, wave_im))
        object_re = patch_cells[0, slice_index]
        object_im = patch_cells[1, slice_index]
        exit_re = wave_re * object_re - wave_im * object_im
        exit_im = wave_re * object_im + wave_im * object_re
        if slice_index + 1 < slice_count:
            spread_re, spread_im = transform(exit_re, exit_im, forward_re, forward_im, False)
            turned_re = spread_re * chirp_re - spread_im * chirp_im
            turned_im = spread_re * chirp_im + spread_im * chirp_re
            wave_re, wave_im = transform(turned_re, turned_im, forward_re, forward_im, True)
    far_re, far_im = transform(exit_re, exit_im, forward_re, forward_im, False)
    intensity = jnp.sum(far_re * far_re + far_im * far_im, axis=0)
    modulus_ratio = 1.0 - amplitude / jnp.maximum(jnp.sqrt(intensity), AMPLITUDE_FLOOR)
    back_re, back_im = transform(
        far_re * modulus_ratio, far_im * modulus_ratio, forward_re, forward_im, True
    )
    object_terms = [None] * slice_count
    for slice_index in reversed(range(slice_count)):
        wave_re, wave_im = incoming[slice_index]
        object_re = patch_cells[0, slice_index]
        object_im = patch_cells[1, slice_index]
        term_re = jnp.sum(wave_re * back_re + wave_im * back_im, axis=0)
        term_im = jnp.sum(wave_re * back_im - wave_im * back_re, axis=0)
        object_terms[slice_index] = (term_re, term_im)
        inner_re = object_re * back_re + object_im * back_im
        inner_im = object_re * back_im - object_im * back_re
        if slice_index > 0:
            spread_re, spread_im = transform(inner_re, inner_im, forward_re, forward_im, False)
            turned_re = spread_re * chirp_re + spread_im * chirp_im
            turned_im = spread_im * chirp_re - spread_re * chirp_im
            back_re, back_im = transform(turned_re, turned_im, forward_re, forward_im, True)
    object_stack = jnp.stack(
        [
            jnp.stack([pair_terms[0] for pair_terms in object_terms]),
            jnp.stack([pair_terms[1] for pair_terms in object_terms]),
        ]
    )
    probe_stack = jnp.stack([inner_re, inner_im])
    return (object_stack, probe_stack)


def column_strip(piece, offset):
    return from_behind(piece, "col", offset)


def row_strip(piece, offset):
    return from_behind(piece, "row", offset)


def return_sectioned(gradient, rim_width, tile_cells):
    rim_start = rim_width + tile_cells
    rim_end = tile_cells - rim_width
    from_left = column_strip(gradient[:, :, :, rim_start:], 1)
    from_right = column_strip(gradient[:, :, :, :rim_width], -1)
    middle = gradient[:, :, :, rim_width:rim_start]
    middle = middle.at[:, :, :, :rim_width].add(from_left)
    middle = middle.at[:, :, :, rim_end:].add(from_right)
    from_above = row_strip(middle[:, :, rim_start:, :], 1)
    from_below = row_strip(middle[:, :, :rim_width, :], -1)
    tile_grad = middle[:, :, rim_width:rim_start, :]
    tile_grad = tile_grad.at[:, :, :rim_width, :].add(from_above)
    tile_grad = tile_grad.at[:, :, rim_end:, :].add(from_below)
    return tile_grad


def body(object_field, probe_modes, amplitudes, offsets, counts):
    pattern_side = probe_modes.shape[-1]
    rim_width = pattern_side // 2
    slice_count = object_field.shape[1]
    tile_cells = object_field.shape[-1]
    slot_count = amplitudes.shape[1]
    ext_side = tile_cells + 2 * rim_width
    dft_table = tables(pattern_side)
    current = object_field
    probe_total = jnp.zeros(probe_modes.shape, jnp.float32)
    for batch_index in range(amplitudes.shape[0]):
        extended = with_halo(current, (("row", 2), ("col", 3)), rim_width)
        batch_amplitudes = amplitudes[batch_index, :, 0]
        batch_rows = offsets[batch_index, 0, :, 0]
        batch_cols = offsets[batch_index, 1, :, 0]
        slot_limit = counts[batch_index, 0, 0]

        def slot_terms(slot_index):
            start_row = batch_rows[slot_index]
            start_col = batch_cols[slot_index]
            zero_index = jnp.zeros((), jnp.int32)
            anchor = (zero_index, zero_index, start_row, start_col)
            patch_cells = lax.dynamic_slice(
                extended, anchor, (2, slice_count, pattern_side, pattern_side)
            )
            amplitude = lax.dynamic_index_in_dim(batch_amplitudes, slot_index, 0, keepdims=False)
            object_stack, probe_stack = position_terms(
                patch_cells, probe_modes, amplitude, dft_table
            )
            return (anchor, object_stack, probe_stack)

        def accumulate(running, anchor, object_stack, probe_stack):
            gradient, probe_part = running
            window = lax.dynamic_slice(gradient, anchor, object_stack.shape)
            gradient = lax.dynamic_update_slice(gradient, window + object_stack, anchor)
            return (gradient, probe_part + probe_stack)

        def visit_masked(slot_index, running):
            anchor, object_stack, probe_stack = slot_terms(slot_index)
            weight = (slot_index < slot_limit).astype(jnp.float32)
            return accumulate(running, anchor, object_stack * weight, probe_stack * weight)

        running = (
            jnp.zeros((2, slice_count, ext_side, ext_side), jnp.float32),
            jnp.zeros(probe_modes.shape, jnp.float32),
        )
        running = lax.fori_loop(0, slot_count, visit_masked, running)
        gradient, probe_part = running
        tile_grad = return_sectioned(gradient, rim_width, tile_cells)
        current = current - OBJECT_STEP * tile_grad
        probe_total = probe_total + lax.psum(probe_part, ("row", "col"))
    return (current, probe_modes - PROBE_STEP * probe_total)


def solution(mesh):
    return jax.shard_map(
        body,
        mesh=mesh,
        in_specs=(
            P(None, None, "row", "col"),
            P(),
            P(None, "row", "col", None, None),
            P(None, None, "row", "col"),
            P(None, "row", "col"),
        ),
        out_specs=(P(None, None, "row", "col"), P()),
        check_vma=False,
    )
```

profile of v0, /device:TPU:1, one launch (start us, length us, event | category | flops | bytes accessed | tf_op | source)
XLA Modules:
  0.0 909.7 jit_solution(2415965093989044361)
XLA Ops:
  8.9 5.7 collective-permute-start
  16.0 9.1 collective-permute-done
  25.1 13.4 %collective-permute-done.1 = f32[2,2,128,256]{2,3,1,0:T(8,128)S(1)} collective-permute-done((f32[2,2,128,256]{2,3,1,0:T(8,128)S(1)}, f32[2,2,128,256]{2,3,1,0:T(8,128)S(1)}, u32[]{:S(2)}, u32[]{:S(2)}) %collective-permute-start.1) | collective-permute-done | bytes 524320 | tf_op jit(solution)/shard_map/ppermute | solution.py:26
  40.3 4.7 collective-permute-start.2
  45.0 1.9 collective-permute-start.3
  47.3 2.7 fusion.773
  52.7 4.3 collective-permute-done.2
  57.0 4.4 collective-permute-done.3
  61.4 4.1 pad_maximum_fusion
  65.5 2.6 broadcast.240.clone2
  68.1 272.4 %while.46 = (s32[]{:T(128)}, f32[2,2,512,512]{3,2,1,0:T(8,128)}, f32[2,2,256,256]{2,3,1,0:T(8,128)}, s32[3]{0:T(128)S(1)}, s32[3]{0:T(128)S(1)}, /*index=5*/f32[...) while((s32[]{:T(128)}, f32[2,2,512,512]{3,2,1,0:T(8,128)}, ...), condition=%wide.region_6.7_spmd.clone.clone.clone.clone, body=%wide.region_0.6_spmd.clone.clone.clone.clone.sunk | while | flops 3292069888 | bytes 88081760 | solution.py:187
  75.4 1.7 dynamic-slice_bitcast_fusion.5
  134.8 2.4 add_bitcast_fusion.4
  138.9 1.8 constant_dynamic-slice_fusion.8
  141.0 3.1 fusion.1267
  145.7 12.0 %dynamic_update_slice.24 = f32[2,2,512,512]{3,2,1,0:T(8,128)} dynamic-update-slice(f32[2,2,512,512]{3,2,1,0:T(8,128)} %get-tuple-element.1607, f32[2,2,256,256]{3,2,1,0:T(8,128)S(1)} %copy.239, s32[]{:T(128)} %constant.326.clone.1..sunk, s32[]{:T(128)} %constant.326.clone.1..sunk, s32[]{:T(128)S(6)} %select_n.701, s32[]{:T(128)S(6)} %select_n.702) | dynamic-update-slice | bytes 2097156 | tf_op jit(solution)/shard_map/while/body/eval_jaxpr/dynamic_update_slice | solution.py:175
  164.7 1.7 dynamic-slice_bitcast_fusion.5
  224.4 2.4 add_bitcast_fusion.4
  228.4 1.8 constant_dynamic-slice_fusion.8
  230.6 3.5 fusion.1267
  235.6 11.7 %dynamic_update_slice.24 = f32[2,2,512,512]{3,2,1,0:T(8,128)} dynamic-update-slice(f32[2,2,512,512]{3,2,1,0:T(8,128)} %get-tuple-element.1607, f32[2,2,256,256]{3,2,1,0:T(8,128)S(1)} %copy.239, s32[]{:T(128)} %constant.326.clone.1..sunk, s32[]{:T(128)} %constant.326.clone.1..sunk, s32[]{:T(128)S(6)} %select_n.701, s32[]{:T(128)S(6)} %select_n.702) | dynamic-update-slice | bytes 2097156 | tf_op jit(solution)/shard_map/while/body/eval_jaxpr/dynamic_update_slice | solution.py:175
  313.7 2.4 add_bitcast_fusion.4
  317.8 1.8 constant_dynamic-slice_fusion.8
  319.9 3.5 fusion.1267
  325.0 11.9 %dynamic_update_slice.24 = f32[2,2,512,512]{3,2,1,0:T(8,128)} dynamic-update-slice(f32[2,2,512,512]{3,2,1,0:T(8,128)} %get-tuple-element.1607, f32[2,2,256,256]{3,2,1,0:T(8,128)S(1)} %copy.239, s32[]{:T(128)} %constant.326.clone.1..sunk, s32[]{:T(128)} %constant.326.clone.1..sunk, s32[]{:T(128)S(6)} %select_n.701, s32[]{:T(128)S(6)} %select_n.702) | dynamic-update-slice | bytes 2097156 | tf_op jit(solution)/shard_map/while/body/eval_jaxpr/dynamic_update_slice | solution.py:175
  340.5 1.9 fusion.768
  342.3 2.1 collective-permute-start.4
  344.4 2.5 collective-permute-start.5
  347.1 9.0 collective-permute-done.4
  356.3 4.2 collective-permute-done.5
  360.8 5.6 collective-permute-start.6
  367.9 4.7 collective-permute-done.6
  372.6 13.3 %collective-permute-done.7 = f32[2,2,128,256]{3,2,1,0:T(8,128)S(1)} collective-permute-done((f32[2,2,128,256]{3,2,1,0:T(8,128)S(1)}, f32[2,2,128,256]{3,2,1,0:T(8,128)S(1)}, u32[]{:S(2)}, u32[]{:S(2)}) %collective-permute-start.7) | collective-permute-done | bytes 524320 | tf_op jit(solution)/shard_map/ppermute | solution.py:15
  386.3 4.7 collective-permute-start.8
  392.4 6.5 collective-permute-done.8
  398.9 14.4 %collective-permute-done.9 = f32[2,2,128,256]{3,2,1,0:T(8,128)S(1)} collective-permute-done((f32[2,2,128,256]{3,2,1,0:T(8,128)S(1)}, f32[2,2,128,256]{3,2,1,0:T(8,128)S(1)}, u32[]{:S(2)}, u32[]{:S(2)}) %collective-permute-start.9) | collective-permute-done | bytes 524320 | tf_op jit(solution)/shard_map/ppermute | solution.py:26
  415.0 9.9 %collective-permute-start.10 = (f32[2,2,512,128]{3,2,1,0:T(8,128)}, f32[2,2,512,128]{3,2,1,0:T(8,128)}, u32[]{:S(2)}, u32[]{:S(2)}) collective-permute-start(f32[2,2,512,128]{3,2,1,0:T(8,128)} %get-tuple-element.1344), channel_id=1, source_target_pairs={{0,1},{1,2},{2,3},{3,4},{4,5},{5,6},{6,7},{7,8},{8,9},{9,10},{10,1... | collective-permute-start | bytes 3145736 | tf_op jit(solution)/shard_map/ppermute | solution.py:25
  424.9 1.9 collective-permute-start.11
  428.0 8.9 collective-permute-done.10
  437.0 4.4 collective-permute-done.11
  441.4 4.1 pad_maximum_fusion.1
  445.5 2.6 broadcast.240.clone
  448.1 273.8 %while.47 = (s32[]{:T(128)}, f32[2,2,512,512]{3,2,1,0:T(8,128)}, f32[2,2,256,256]{2,3,1,0:T(8,128)}, s32[3]{0:T(128)S(1)}, s32[3]{0:T(128)S(1)}, /*index=5*/f32[...) while((s32[]{:T(128)}, f32[2,2,512,512]{3,2,1,0:T(8,128)}, ...), condition=%wide.region_13.14_spmd.clone.clone.clone.clone, body=%wide.region_7.13_spmd.clone.clone.clone.clone.sunk | while | flops 3292069888 | bytes 83887400 | solution.py:187
  515.6 2.4 add_bitcast_fusion.5
  519.7 1.8 constant_dynamic-slice_fusion.9
  521.8 3.2 fusion.1400
  526.6 11.6 %dynamic_update_slice.25 = f32[2,2,512,512]{3,2,1,0:T(8,128)} dynamic-update-slice(f32[2,2,512,512]{3,2,1,0:T(8,128)} %get-tuple-element.1649, f32[2,2,256,256]{3,2,1,0:T(8,128)S(1)} %copy.245, s32[]{:T(128)} %constant.326.clone.1..sunk.1, s32[]{:T(128)} %constant.326.clone.1..sunk.1, s32[]{:T(128)S(6)} %select_n.752, s32[]{:T(128)S(6)} %select_n.753) | dynamic-update-slice | bytes 2097156 | tf_op jit(solution)/shard_map/while/body/eval_jaxpr/dynamic_update_slice | solution.py:175
  605.5 2.4 add_bitcast_fusion.5
  609.7 1.8 constant_dynamic-slice_fusion.9
  611.8 3.5 fusion.1400
  616.9 11.9 %dynamic_update_slice.25 = f32[2,2,512,512]{3,2,1,0:T(8,128)} dynamic-update-slice(f32[2,2,512,512]{3,2,1,0:T(8,128)} %get-tuple-element.1649, f32[2,2,256,256]{3,2,1,0:T(8,128)S(1)} %copy.245, s32[]{:T(128)} %constant.326.clone.1..sunk.1, s32[]{:T(128)} %constant.326.clone.1..sunk.1, s32[]{:T(128)S(6)} %select_n.752, s32[]{:T(128)S(6)} %select_n.753) | dynamic-update-slice | bytes 2097156 | tf_op jit(solution)/shard_map/while/body/eval_jaxpr/dynamic_update_slice | solution.py:175
  696.3 2.4 add_bitcast_fusion.5
  700.4 1.8 constant_dynamic-slice_fusion.9
  702.5 3.5 fusion.1400
  707.6 11.6 %dynamic_update_slice.25 = f32[2,2,512,512]{3,2,1,0:T(8,128)} dynamic-update-slice(f32[2,2,512,512]{3,2,1,0:T(8,128)} %get-tuple-element.1649, f32[2,2,256,256]{3,2,1,0:T(8,128)S(1)} %copy.245, s32[]{:T(128)} %constant.326.clone.1..sunk.1, s32[]{:T(128)} %constant.326.clone.1..sunk.1, s32[]{:T(128)S(6)} %select_n.752, s32[]{:T(128)S(6)} %select_n.753) | dynamic-update-slice | bytes 2097156 | tf_op jit(solution)/shard_map/while/body/eval_jaxpr/dynamic_update_slice | solution.py:175
  721.9 3.1 fusion.767
  725.0 2.1 collective-permute-start.12
  727.2 3.3 collective-permute-start.13
  731.8 3.2 slice.438
  736.3 2.5 add.859
  740.9 2.7 collective-permute-done.13
  746.1 6.2 collective-permute-start.14
  753.7 142.7 %all-reduce.2.cloned.1.call-done = f32[2,2,256,256]{3,2,1,0:T(8,128)} async-done(((f32[2,2,256,256]{3,2,1,0:T(8,128)}), f32[2,2,256,256]{3,2,1,0:T(8,128)}) %all-reduce.2.cloned.1.call-update) | async-done | bytes 1048592 | tf_op jit(solution)/shard_map/psum | solution.py:191
  896.5 2.6 multiply_subtract_fusion
  (441 shorter events, 418.8 us)
Async XLA Ops:
  7.2 889.3 %all-reduce.2.cloned.1.call-start = ((), (), s32[]{:S(2)}) async-start(), calls=%async_computation | async-start | bytes 2097152 | tf_op jit(solution)/shard_map/psum | solution.py:191
  8.9 16.2 %collective-permute-start = (f32[2,2,128,256]{2,3,1,0:T(8,128)S(1)}, f32[2,2,128,256]{2,3,1,0:T(8,128)S(1)}, u32[]{:S(2)}, u32[]{:S(2)}) collective-permute-start(f32[2,2,128,256]{2,3,1,0:T(8,128)S(1)} %get-tuple-element.1354), channel_id=1, source_target_pairs={{0,16},{16,32},{32,48},{48,64},{64,80},{80,96},{96,112},{1,17},{17... | collective-permute-start | bytes 1572872 | tf_op jit(solution)/shard_map/ppermute | solution.py:25
  14.5 32.4 %copy-start.9 = (f32[2,2,256,256]{3,2,1,0:T(8,128)S(1)}, f32[2,2,256,256]{3,2,1,0:T(8,128)}, u32[]{:S(2)}) copy-start(f32[2,2,256,256]{3,2,1,0:T(8,128)} %param.26) | copy-start | bytes 3145732
  14.6 23.9 %collective-permute-start.1 = (f32[2,2,128,256]{2,3,1,0:T(8,128)S(1)}, f32[2,2,128,256]{2,3,1,0:T(8,128)S(1)}, u32[]{:S(2)}, u32[]{:S(2)}) collective-permute-start(f32[2,2,128,256]{2,3,1,0:T(8,128)S(1)} %get-tuple-element.1355), channel_id=1, source_target_pairs={{16,0},{32,16},{48,32},{64,48},{80,64},{96,80},{112,96},{17,1},{33... | collective-permute-start | bytes 1572872 | tf_op jit(solution)/shard_map/ppermute | solution.py:26
  25.1 15.2 %copy-start.12 = (f32[2,2,128,256]{2,3,1,0:T(8,128)}, f32[2,2,128,256]{2,3,1,0:T(8,128)S(1)}, u32[]{:S(2)}) copy-start(f32[2,2,128,256]{2,3,1,0:T(8,128)S(1)} %collective-permute-done) | copy-start | bytes 1572868
  38.5 1.8 copy-start.14
  40.3 11.2 %copy-start.17 = (s32[2,1,1]{0,2,1:T(1,128)S(1)}, s32[2,1,1]{0,2,1:T(1,128)}, u32[]{:S(2)}) copy-start(s32[2,1,1]{0,2,1:T(1,128)} %param.29) | copy-start | bytes 28
  40.3 11.8 %copy-start.16 = (s32[2,2,3,1]{2,3,1,0:T(1,128)S(1)}, s32[2,2,3,1]{2,3,1,0:T(1,128)}, u32[]{:S(2)}) copy-start(s32[2,2,3,1]{2,3,1,0:T(1,128)} %param.28) | copy-start | bytes 148
  40.3 16.7 %collective-permute-start.2 = (f32[2,2,512,128]{2,3,1,0:T(8,128)}, f32[2,2,512,128]{2,3,1,0:T(8,128)}, u32[]{:S(2)}, u32[]{:S(2)}) collective-permute-start(f32[2,2,512,128]{2,3,1,0:T(8,128)} %get-tuple-element.1348), channel_id=1, source_target_pairs={{0,1},{1,2},{2,3},{3,4},{4,5},{5,6},{6,7},{7,8},{8,9},{9,10},{10,1... | collective-permute-start | bytes 3145736 | tf_op jit(solution)/shard_map/ppermute | solution.py:25
  45.0 16.4 %collective-permute-start.3 = (f32[2,2,512,128]{2,3,1,0:T(8,128)}, f32[2,2,512,128]{2,3,1,0:T(8,128)}, u32[]{:S(2)}, u32[]{:S(2)}) collective-permute-start(f32[2,2,512,128]{2,3,1,0:T(8,128)} %get-tuple-element.1349), channel_id=1, source_target_pairs={{1,0},{2,1},{3,2},{4,3},{5,4},{6,5},{7,6},{8,7},{9,8},{10,9},{11,1... | collective-permute-start | bytes 3145736 | tf_op jit(solution)/shard_map/ppermute | solution.py:26
  47.3 14.1 %copy-start.13 = (f32[2,2,128,256]{2,3,1,0:T(8,128)S(1)}, f32[2,2,128,256]{2,3,1,0:T(8,128)}, u32[]{:S(2)}) copy-start(f32[2,2,128,256]{2,3,1,0:T(8,128)} %copy-done.12) | copy-start | bytes 1572868
  68.6 37.8 %copy-start.6 = (f32[3,256,256]{1,2,0:T(8,128)}, f32[3,256,256]{1,2,0:T(8,128)S(1)}, u32[]{:S(2)}) copy-start(f32[3,256,256]{1,2,0:T(8,128)S(1)} %get-tuple-element.1627) | copy-start | bytes 2359300 | tf_op jit(solution)/shard_map/while
  144.1 13.6 %copy-start.7 = (f32[3,256,256]{1,2,0:T(8,128)S(1)}, f32[3,256,256]{1,2,0:T(8,128)}, u32[]{:S(2)}) copy-start(f32[3,256,256]{1,2,0:T(8,128)} %copy-done.6) | copy-start | bytes 2359300 | tf_op jit(solution)/shard_map/while
  157.9 38.0 %copy-start.6 = (f32[3,256,256]{1,2,0:T(8,128)}, f32[3,256,256]{1,2,0:T(8,128)S(1)}, u32[]{:S(2)}) copy-start(f32[3,256,256]{1,2,0:T(8,128)S(1)} %get-tuple-element.1627) | copy-start | bytes 2359300 | tf_op jit(solution)/shard_map/while
  234.0 13.3 %copy-start.7 = (f32[3,256,256]{1,2,0:T(8,128)S(1)}, f32[3,256,256]{1,2,0:T(8,128)}, u32[]{:S(2)}) copy-start(f32[3,256,256]{1,2,0:T(8,128)} %copy-done.6) | copy-start | bytes 2359300 | tf_op jit(solution)/shard_map/while
  247.5 38.0 %copy-start.6 = (f32[3,256,256]{1,2,0:T(8,128)}, f32[3,256,256]{1,2,0:T(8,128)S(1)}, u32[]{:S(2)}) copy-start(f32[3,256,256]{1,2,0:T(8,128)S(1)} %get-tuple-element.1627) | copy-start | bytes 2359300 | tf_op jit(solution)/shard_map/while
  323.4 13.6 %copy-start.7 = (f32[3,256,256]{1,2,0:T(8,128)S(1)}, f32[3,256,256]{1,2,0:T(8,128)}, u32[]{:S(2)}) copy-start(f32[3,256,256]{1,2,0:T(8,128)} %copy-done.6) | copy-start | bytes 2359300 | tf_op jit(solution)/shard_map/while
  340.5 6.4 copy-start
  342.3 13.8 %collective-permute-start.4 = (f32[2,2,512,128]{3,2,1,0:T(8,128)S(1)}, f32[2,2,512,128]{3,2,1,0:T(8,128)S(1)}, u32[]{:S(2)}, u32[]{:S(2)}) collective-permute-start(f32[2,2,512,128]{3,2,1,0:T(8,128)S(1)} %get-tuple-element.1341), channel_id=1, source_target_pairs={{0,1},{1,2},{2,3},{3,4},{4,5},{5,6},{6,7},{7,8},{8,9},{9,10},{10,1... | collective-permute-start | bytes 3145736 | tf_op jit(solution)/shard_map/ppermute | solution.py:15
  344.4 16.1 %collective-permute-start.5 = (f32[2,2,512,128]{3,2,1,0:T(8,128)S(1)}, f32[2,2,512,128]{3,2,1,0:T(8,128)S(1)}, u32[]{:S(2)}, u32[]{:S(2)}) collective-permute-start(f32[2,2,512,128]{3,2,1,0:T(8,128)S(1)} %get-tuple-element.1340), channel_id=1, source_target_pairs={{1,0},{2,1},{3,2},{4,3},{5,4},{6,5},{7,6},{8,7},{9,8},{10,9},{11,1... | collective-permute-start | bytes 3145736 | tf_op jit(solution)/shard_map/ppermute | solution.py:15
  360.7 25.3 %copy-start.8 = (f32[2,2,256,256]{3,2,1,0:T(8,128)S(1)}, f32[2,2,256,256]{3,2,1,0:T(8,128)}, u32[]{:S(2)}) copy-start(f32[2,2,256,256]{3,2,1,0:T(8,128)} %param.25) | copy-start | bytes 3145732
  360.8 11.7 %collective-permute-start.6 = (f32[2,2,128,256]{3,2,1,0:T(8,128)S(1)}, f32[2,2,128,256]{3,2,1,0:T(8,128)S(1)}, u32[]{:S(2)}, u32[]{:S(2)}) collective-permute-start(f32[2,2,128,256]{3,2,1,0:T(8,128)S(1)} %get-tuple-element.1347), channel_id=1, source_target_pairs={{0,16},{16,32},{32,48},{48,64},{64,80},{80,96},{96,112},{1,17},{17... | collective-permute-start | bytes 1572872 | tf_op jit(solution)/shard_map/ppermute | solution.py:15
  366.5 19.4 %collective-permute-start.7 = (f32[2,2,128,256]{3,2,1,0:T(8,128)S(1)}, f32[2,2,128,256]{3,2,1,0:T(8,128)S(1)}, u32[]{:S(2)}, u32[]{:S(2)}) collective-permute-start(f32[2,2,128,256]{3,2,1,0:T(8,128)S(1)} %get-tuple-element.1346), channel_id=1, source_target_pairs={{16,0},{32,16},{48,32},{64,48},{80,64},{96,80},{112,96},{17,1},{33... | collective-permute-start | bytes 1572872 | tf_op jit(solution)/shard_map/ppermute | solution.py:15
  386.2 55.2 %copy-start.3 = (f32[2,2,256,256]{3,2,1,0:T(8,128)}, f32[2,2,256,256]{3,2,1,0:T(8,128)S(1)}, u32[]{:S(2)}) copy-start(f32[2,2,256,256]{3,2,1,0:T(8,128)S(1)} %multiply_subtract_fusion.2) | copy-start | bytes 3145732
  386.3 12.7 %collective-permute-start.8 = (f32[2,2,128,256]{3,2,1,0:T(8,128)S(1)}, f32[2,2,128,256]{3,2,1,0:T(8,128)S(1)}, u32[]{:S(2)}, u32[]{:S(2)}) collective-permute-start(f32[2,2,128,256]{3,2,1,0:T(8,128)S(1)} %get-tuple-element.1352), channel_id=1, source_target_pairs={{0,16},{16,32},{32,48},{48,64},{64,80},{80,96},{96,112},{1,17},{17... | collective-permute-start | bytes 1572872 | tf_op jit(solution)/shard_map/ppermute | solution.py:25
  391.0 35.9 %copy-start.11 = (f32[1,3,1,256,256]{4,3,2,1,0:T(8,128)S(1)}, f32[1,3,1,256,256]{4,3,2,1,0:T(8,128)}, u32[]{:S(2)}) copy-start(f32[1,3,1,256,256]{4,3,2,1,0:T(8,128)} %get-tuple-element.1350) | copy-start | bytes 2359300
  391.0 22.3 %collective-permute-start.9 = (f32[2,2,128,256]{3,2,1,0:T(8,128)S(1)}, f32[2,2,128,256]{3,2,1,0:T(8,128)S(1)}, u32[]{:S(2)}, u32[]{:S(2)}) collective-permute-start(f32[2,2,128,256]{3,2,1,0:T(8,128)S(1)} %get-tuple-element.1353), channel_id=1, source_target_pairs={{16,0},{32,16},{48,32},{64,48},{80,64},{96,80},{112,96},{17,1},{33... | collective-permute-start | bytes 1572872 | tf_op jit(solution)/shard_map/ppermute | solution.py:26
  413.3 1.7 copy-start.15
  415.0 21.9 %collective-permute-start.10 = (f32[2,2,512,128]{3,2,1,0:T(8,128)}, f32[2,2,512,128]{3,2,1,0:T(8,128)}, u32[]{:S(2)}, u32[]{:S(2)}) collective-permute-start(f32[2,2,512,128]{3,2,1,0:T(8,128)} %get-tuple-element.1344), channel_id=1, source_target_pairs={{0,1},{1,2},{2,3},{3,4},{4,5},{5,6},{6,7},{7,8},{8,9},{9,10},{10,1... | collective-permute-start | bytes 3145736 | tf_op jit(solution)/shard_map/ppermute | solution.py:25
  424.9 16.4 %collective-permute-start.11 = (f32[2,2,512,128]{3,2,1,0:T(8,128)}, f32[2,2,512,128]{3,2,1,0:T(8,128)}, u32[]{:S(2)}, u32[]{:S(2)}) collective-permute-start(f32[2,2,512,128]{3,2,1,0:T(8,128)} %get-tuple-element.1345), channel_id=1, source_target_pairs={{1,0},{2,1},{3,2},{4,3},{5,4},{6,5},{7,6},{8,7},{9,8},{10,9},{11,1... | collective-permute-start | bytes 3145736 | tf_op jit(solution)/shard_map/ppermute | solution.py:26
  445.5 2.6 copy-start.18
  445.5 2.6 copy-start.19
  721.9 8.6 copy-start.1
  725.0 9.9 %copy-start.2 = (f32[2,2,256,256]{2,3,1,0:T(8,128)S(1)}, f32[2,2,256,256]{2,3,1,0:T(8,128)}, u32[]{:S(2)}) copy-start(f32[2,2,256,256]{2,3,1,0:T(8,128)} %get-tuple-element.843) | copy-start | bytes 3145732
  725.0 14.2 %collective-permute-start.12 = (f32[2,2,512,128]{3,2,1,0:T(8,128)}, f32[2,2,512,128]{3,2,1,0:T(8,128)}, u32[]{:S(2)}, u32[]{:S(2)}) collective-permute-start(f32[2,2,512,128]{3,2,1,0:T(8,128)} %get-tuple-element.1339), channel_id=1, source_target_pairs={{0,1},{1,2},{2,3},{3,4},{4,5},{5,6},{6,7},{7,8},{8,9},{9,10},{10,1... | collective-permute-start | bytes 3145736 | tf_op jit(solution)/shard_map/ppermute | solution.py:15
  727.2 16.4 %collective-permute-start.13 = (f32[2,2,512,128]{3,2,1,0:T(8,128)}, f32[2,2,512,128]{3,2,1,0:T(8,128)}, u32[]{:S(2)}, u32[]{:S(2)}) collective-permute-start(f32[2,2,512,128]{3,2,1,0:T(8,128)} %get-tuple-element.1338), channel_id=1, source_target_pairs={{1,0},{2,1},{3,2},{4,3},{5,4},{6,5},{7,6},{8,7},{9,8},{10,9},{11,1... | collective-permute-start | bytes 3145736 | tf_op jit(solution)/shard_map/ppermute | solution.py:15
  731.8 4.5 copy-start.10
  736.3 2.9 copy-start.5
  746.1 153.1 %collective-permute-start.14 = (f32[2,2,128,256]{3,2,1,0:T(8,128)}, f32[2,2,128,256]{3,2,1,0:T(8,128)}, u32[]{:S(2)}, u32[]{:S(2)}) collective-permute-start(f32[2,2,128,256]{3,2,1,0:T(8,128)} %get-tuple-element.1343), channel_id=1, source_target_pairs={{0,16},{16,32},{32,48},{48,64},{64,80},{80,96},{96,112},{1,17},{17... | collective-permute-start | bytes 1572872 | tf_op jit(solution)/shard_map/ppermute | solution.py:15
  752.3 149.2 %copy-start.4 = (f32[2,2,256,256]{3,2,1,0:T(8,128)S(1)}, f32[2,2,256,256]{3,2,1,0:T(8,128)}, u32[]{:S(2)}) copy-start(f32[2,2,256,256]{3,2,1,0:T(8,128)} %copy-done.3) | copy-start | bytes 3145732
  752.3 148.0 %collective-permute-start.15 = (f32[2,2,128,256]{3,2,1,0:T(8,128)}, f32[2,2,128,256]{3,2,1,0:T(8,128)}, u32[]{:S(2)}, u32[]{:S(2)}) collective-permute-start(f32[2,2,128,256]{3,2,1,0:T(8,128)} %get-tuple-element.1342), channel_id=1, source_target_pairs={{16,0},{32,16},{48,32},{64,48},{80,64},{96,80},{112,96},{17,1},{33... | collective-permute-start | bytes 1572872 | tf_op jit(solution)/shard_map/ppermute | solution.py:15
Sparse Core Ops, SparseCore 0:
  738.9 157.5 all-reduce.1
where the time goes:
time: 916 us; the launch traced here: 910 us
  matrix products  358 us (39%)
  waiting for transfers between devices  243 us (27%)
  local copies, waits for them, and re-layouts  141 us (15%)
  other arithmetic  62.3 us (7%)
  starting transfers between devices  56.1 us (6%)
  loops' own time  34.6 us (4%)
  between operations  14.7 us (2%)
    dot_general x288, matrix products, contract(): return jnp.einsum(form, left, right, preferred_element_type=jnp.float32)  358 us
    psum x1, waiting for transfers between devices, body(): probe_total = probe_total + lax.psum(probe_part, ('row', 'col'))  143 us
    dynamic_update_slice x12, local copies, waits for them, and re-layouts, accumulate(): gradient = lax.dynamic_update_slice(gradient, window + object_stack, anchor)  80.3 us
    ppermute x4, waiting for transfers between devices, with_halo(): after = lax.ppermute(leading, axis, down)  36.6 us
    another operation x2, loops' own time, body(): running = lax.fori_loop(0, slot_count, visit_masked, running)  34.6 us
    ppermute x8, waiting for transfers between devices, from_behind(): lax.ppermute(value, axis, [(source, source + steps) for source in range(l...  34.3 us
    ppermute x4, waiting for transfers between devices, with_halo(): before = lax.ppermute(last, axis, up)  28.9 us
    ppermute x4, starting transfers between devices, with_halo(): before = lax.ppermute(last, axis, up)  24.9 us
  transfers between devices with their start and end apart: 17, of which 15 were waited for; matrix products, arithmetic and copies ran while one was open for 3% of the time, Pallas kernels for 0%

commit v1 on v0

--- a/solution.py
+++ b/solution.py
@@ -188,7 +188,7 @@
         gradient, probe_part = running
         tile_grad = return_sectioned(gradient, rim_width, tile_cells)
         current = current - OBJECT_STEP * tile_grad
-        probe_total = probe_total + lax.psum(probe_part, ("row", "col"))
+        probe_total = probe_total + lax.psum(lax.psum(probe_part, "row"), "col")
     return (current, probe_modes - PROBE_STEP * probe_total)
 
 

time: 916 us -> 972 us (1.061)
  waiting for transfers between devices: 243 us -> 297 us
    psum x1 -> x2, waiting for transfers between devices: 143 us -> 197 us  [body(): probe_total = probe_total + lax.psum(lax.psum(probe_part, 'row'), 'col')]
  transfers between devices with their start and end apart: 17 -> 18, of which waited for: 15 -> 16; matrix products, arithmetic and copies ran while one was open for 3% -> 2% of each run, Pallas kernels for 0% -> 0%
where the time goes in v1:
time: 972 us; the launch traced here: 966 us
  matrix products  358 us (37%)
  waiting for transfers between devices  297 us (31%)
  local copies, waits for them, and re-layouts  141 us (15%)
  other arithmetic  62.1 us (6%)
  starting transfers between devices  55.9 us (6%)
  loops' own time  36.3 us (4%)
  between operations  14.8 us (2%)
    dot_general x288, matrix products, contract(): return jnp.einsum(form, left, right, preferred_element_type=jnp.float32)  358 us
    psum x2, waiting for transfers between devices, body(): probe_total = probe_total + lax.psum(lax.psum(probe_part, 'row'), 'col')  197 us
    dynamic_update_slice x12, local copies, waits for them, and re-layouts, accumulate(): gradient = lax.dynamic_update_slice(gradient, window + object_stack, anchor)  80.3 us
    ppermute x4, waiting for transfers between devices, with_halo(): after = lax.ppermute(leading, axis, down)  36.7 us
    another operation x2, loops' own time, body(): running = lax.fori_loop(0, slot_count, visit_masked, running)  36.3 us
    ppermute x8, waiting for transfers between devices, from_behind(): lax.ppermute(value, axis, [(source, source + steps) for source in range(l...  34.3 us
    ppermute x4, waiting for transfers between devices, with_halo(): before = lax.ppermute(last, axis, up)  28.8 us
    ppermute x4, starting transfers between devices, with_halo(): before = lax.ppermute(last, axis, up)  24.9 us
  transfers between devices with their start and end apart: 18, of which 16 were waited for; matrix products, arithmetic and copies ran while one was open for 2% of the time, Pallas kernels for 0%

profile of v1, /device:TPU:1, one launch (start us, length us, event | category | flops | bytes accessed | tf_op | source)
XLA Modules:
  0.0 965.8 jit_solution(12078481909129152768)
XLA Ops:
  8.9 5.7 collective-permute-start
  16.0 9.1 collective-permute-done
  25.1 13.4 %collective-permute-done.1 = f32[2,2,128,256]{2,3,1,0:T(8,128)S(1)} collective-permute-done((f32[2,2,128,256]{2,3,1,0:T(8,128)S(1)}, f32[2,2,128,256]{2,3,1,0:T(8,128)S(1)}, u32[]{:S(2)}, u32[]{:S(2)}) %collective-permute-start.1) | collective-permute-done | bytes 524320 | tf_op jit(solution)/shard_map/ppermute | solution.py:26
  40.3 4.7 collective-permute-start.2
  45.0 1.9 collective-permute-start.3
  47.3 2.8 fusion.773
  52.7 4.3 collective-permute-done.2
  57.0 4.4 collective-permute-done.3
  61.4 4.1 pad_maximum_fusion
  65.5 2.6 broadcast.240.clone2
  68.1 272.6 %while.46 = (s32[]{:T(128)}, f32[2,2,512,512]{3,2,1,0:T(8,128)}, f32[2,2,256,256]{2,3,1,0:T(8,128)}, s32[3]{0:T(128)S(1)}, s32[3]{0:T(128)S(1)}, /*index=5*/f32[...) while((s32[]{:T(128)}, f32[2,2,512,512]{3,2,1,0:T(8,128)}, ...), condition=%wide.region_6.7_spmd.clone.clone.clone.clone, body=%wide.region_0.6_spmd.clone.clone.clone.clone.sunk | while | flops 3292069888 | bytes 88081760 | solution.py:187
  134.9 2.4 add_bitcast_fusion.4
  138.9 1.8 constant_dynamic-slice_fusion.8
  141.1 3.1 fusion.1267
  145.8 12.0 %dynamic_update_slice.24 = f32[2,2,512,512]{3,2,1,0:T(8,128)} dynamic-update-slice(f32[2,2,512,512]{3,2,1,0:T(8,128)} %get-tuple-element.1607, f32[2,2,256,256]{3,2,1,0:T(8,128)S(1)} %copy.239, s32[]{:T(128)} %constant.326.clone.1..sunk, s32[]{:T(128)} %constant.326.clone.1..sunk, s32[]{:T(128)S(6)} %select_n.701, s32[]{:T(128)S(6)} %select_n.702) | dynamic-update-slice | bytes 2097156 | tf_op jit(solution)/shard_map/while/body/eval_jaxpr/dynamic_update_slice | solution.py:175
  164.8 1.7 dynamic-slice_bitcast_fusion.5
  224.5 2.4 add_bitcast_fusion.4
  228.6 1.8 constant_dynamic-slice_fusion.8
  230.7 3.5 fusion.1267
  235.8 11.7 %dynamic_update_slice.24 = f32[2,2,512,512]{3,2,1,0:T(8,128)} dynamic-update-slice(f32[2,2,512,512]{3,2,1,0:T(8,128)} %get-tuple-element.1607, f32[2,2,256,256]{3,2,1,0:T(8,128)S(1)} %copy.239, s32[]{:T(128)} %constant.326.clone.1..sunk, s32[]{:T(128)} %constant.326.clone.1..sunk, s32[]{:T(128)S(6)} %select_n.701, s32[]{:T(128)S(6)} %select_n.702) | dynamic-update-slice | bytes 2097156 | tf_op jit(solution)/shard_map/while/body/eval_jaxpr/dynamic_update_slice | solution.py:175
  313.9 2.4 add_bitcast_fusion.4
  318.0 1.8 constant_dynamic-slice_fusion.8
  320.1 3.5 fusion.1267
  325.2 11.9 %dynamic_update_slice.24 = f32[2,2,512,512]{3,2,1,0:T(8,128)} dynamic-update-slice(f32[2,2,512,512]{3,2,1,0:T(8,128)} %get-tuple-element.1607, f32[2,2,256,256]{3,2,1,0:T(8,128)S(1)} %copy.239, s32[]{:T(128)} %constant.326.clone.1..sunk, s32[]{:T(128)} %constant.326.clone.1..sunk, s32[]{:T(128)S(6)} %select_n.701, s32[]{:T(128)S(6)} %select_n.702) | dynamic-update-slice | bytes 2097156 | tf_op jit(solution)/shard_map/while/body/eval_jaxpr/dynamic_update_slice | solution.py:175
  340.7 1.9 fusion.768
  342.5 2.1 collective-permute-start.4
  344.6 2.5 collective-permute-start.5
  347.3 9.0 collective-permute-done.4
  356.5 4.2 collective-permute-done.5
  361.0 5.6 collective-permute-start.6
  368.0 4.7 collective-permute-done.6
  372.8 13.3 %collective-permute-done.7 = f32[2,2,128,256]{3,2,1,0:T(8,128)S(1)} collective-permute-done((f32[2,2,128,256]{3,2,1,0:T(8,128)S(1)}, f32[2,2,128,256]{3,2,1,0:T(8,128)S(1)}, u32[]{:S(2)}, u32[]{:S(2)}) %collective-permute-start.7) | collective-permute-done | bytes 524320 | tf_op jit(solution)/shard_map/ppermute | solution.py:15
  386.5 4.7 collective-permute-start.8
  392.6 6.4 collective-permute-done.8
  399.0 14.5 %collective-permute-done.9 = f32[2,2,128,256]{3,2,1,0:T(8,128)S(1)} collective-permute-done((f32[2,2,128,256]{3,2,1,0:T(8,128)S(1)}, f32[2,2,128,256]{3,2,1,0:T(8,128)S(1)}, u32[]{:S(2)}, u32[]{:S(2)}) %collective-permute-start.9) | collective-permute-done | bytes 524320 | tf_op jit(solution)/shard_map/ppermute | solution.py:26
  415.3 9.8 %collective-permute-start.10 = (f32[2,2,512,128]{3,2,1,0:T(8,128)}, f32[2,2,512,128]{3,2,1,0:T(8,128)}, u32[]{:S(2)}, u32[]{:S(2)}) collective-permute-start(f32[2,2,512,128]{3,2,1,0:T(8,128)} %get-tuple-element.1344), channel_id=1, source_target_pairs={{0,1},{1,2},{2,3},{3,4},{4,5},{5,6},{6,7},{7,8},{8,9},{9,10},{10,1... | collective-permute-start | bytes 3145736 | tf_op jit(solution)/shard_map/ppermute | solution.py:25
  425.1 1.9 collective-permute-start.11
  428.2 8.9 collective-permute-done.10
  437.1 4.4 collective-permute-done.11
  441.5 4.1 pad_maximum_fusion.1
  445.7 2.6 broadcast.240.clone
  448.2 275.5 %while.47 = (s32[]{:T(128)}, f32[2,2,512,512]{3,2,1,0:T(8,128)}, f32[2,2,256,256]{2,3,1,0:T(8,128)}, s32[3]{0:T(128)S(1)}, s32[3]{0:T(128)S(1)}, /*index=5*/f32[...) while((s32[]{:T(128)}, f32[2,2,512,512]{3,2,1,0:T(8,128)}, ...), condition=%wide.region_13.14_spmd.clone.clone.clone.clone, body=%wide.region_7.13_spmd.clone.clone.clone.clone.sunk | while | flops 3292069888 | bytes 83887400 | solution.py:187
  516.3 2.4 add_bitcast_fusion.5
  520.5 1.8 constant_dynamic-slice_fusion.9
  522.6 3.2 fusion.1400
  527.3 11.6 %dynamic_update_slice.25 = f32[2,2,512,512]{3,2,1,0:T(8,128)} dynamic-update-slice(f32[2,2,512,512]{3,2,1,0:T(8,128)} %get-tuple-element.1649, f32[2,2,256,256]{3,2,1,0:T(8,128)S(1)} %copy.245, s32[]{:T(128)} %constant.326.clone.1..sunk.1, s32[]{:T(128)} %constant.326.clone.1..sunk.1, s32[]{:T(128)S(6)} %select_n.752, s32[]{:T(128)S(6)} %select_n.753) | dynamic-update-slice | bytes 2097156 | tf_op jit(solution)/shard_map/while/body/eval_jaxpr/dynamic_update_slice | solution.py:175
  606.8 2.4 add_bitcast_fusion.5
  611.0 1.8 constant_dynamic-slice_fusion.9
  613.1 3.5 fusion.1400
  618.2 11.9 %dynamic_update_slice.25 = f32[2,2,512,512]{3,2,1,0:T(8,128)} dynamic-update-slice(f32[2,2,512,512]{3,2,1,0:T(8,128)} %get-tuple-element.1649, f32[2,2,256,256]{3,2,1,0:T(8,128)S(1)} %copy.245, s32[]{:T(128)} %constant.326.clone.1..sunk.1, s32[]{:T(128)} %constant.326.clone.1..sunk.1, s32[]{:T(128)S(6)} %select_n.752, s32[]{:T(128)S(6)} %select_n.753) | dynamic-update-slice | bytes 2097156 | tf_op jit(solution)/shard_map/while/body/eval_jaxpr/dynamic_update_slice | solution.py:175
  698.2 2.4 add_bitcast_fusion.5
  702.3 1.8 constant_dynamic-slice_fusion.9
  704.4 3.5 fusion.1400
  709.5 11.6 %dynamic_update_slice.25 = f32[2,2,512,512]{3,2,1,0:T(8,128)} dynamic-update-slice(f32[2,2,512,512]{3,2,1,0:T(8,128)} %get-tuple-element.1649, f32[2,2,256,256]{3,2,1,0:T(8,128)S(1)} %copy.245, s32[]{:T(128)} %constant.326.clone.1..sunk.1, s32[]{:T(128)} %constant.326.clone.1..sunk.1, s32[]{:T(128)S(6)} %select_n.752, s32[]{:T(128)S(6)} %select_n.753) | dynamic-update-slice | bytes 2097156 | tf_op jit(solution)/shard_map/while/body/eval_jaxpr/dynamic_update_slice | solution.py:175
  723.8 3.1 fusion.767
  726.9 2.1 collective-permute-start.12
  729.0 3.3 collective-permute-start.13
  733.7 3.2 slice.438
  738.2 2.5 add.863
  742.7 2.7 collective-permute-done.13
  748.0 6.2 collective-permute-start.14
  755.5 76.6 %all-reduce.5.cloned.1.call-done = f32[2,2,256,256]{3,2,1,0:T(8,128)} async-done(((f32[2,2,256,256]{3,2,1,0:T(8,128)}), f32[2,2,256,256]{3,2,1,0:T(8,128)}) %all-reduce.5.cloned.1.call-update) | async-done | bytes 1048592 | tf_op jit(solution)/shard_map/psum | solution.py:191
  835.7 120.7 %all-reduce.3.cloned.1.call-done = f32[2,2,256,256]{3,2,1,0:T(8,128)} async-done(((f32[2,2,256,256]{3,2,1,0:T(8,128)}), f32[2,2,256,256]{3,2,1,0:T(8,128)}) %all-reduce.3.cloned.1.call-update) | async-done | bytes 1048592 | tf_op jit(solution)/shard_map/psum | solution.py:191
  956.4 2.3 multiply_subtract_fusion
  (446 shorter events, 420.6 us)
Async XLA Ops:
  7.2 824.9 %all-reduce.5.cloned.1.call-start = ((), (), s32[]{:S(2)}) async-start(), calls=%async_computation.1 | async-start | bytes 2097152 | tf_op jit(solution)/shard_map/psum | solution.py:191
  8.9 16.2 %collective-permute-start = (f32[2,2,128,256]{2,3,1,0:T(8,128)S(1)}, f32[2,2,128,256]{2,3,1,0:T(8,128)S(1)}, u32[]{:S(2)}, u32[]{:S(2)}) collective-permute-start(f32[2,2,128,256]{2,3,1,0:T(8,128)S(1)} %get-tuple-element.1354), channel_id=1, source_target_pairs={{0,16},{16,32},{32,48},{48,64},{64,80},{80,96},{96,112},{1,17},{17... | collective-permute-start | bytes 1572872 | tf_op jit(solution)/shard_map/ppermute | solution.py:25
  14.5 32.4 %copy-start.9 = (f32[2,2,256,256]{3,2,1,0:T(8,128)S(1)}, f32[2,2,256,256]{3,2,1,0:T(8,128)}, u32[]{:S(2)}) copy-start(f32[2,2,256,256]{3,2,1,0:T(8,128)} %param.26) | copy-start | bytes 3145732
  14.6 23.9 %collective-permute-start.1 = (f32[2,2,128,256]{2,3,1,0:T(8,128)S(1)}, f32[2,2,128,256]{2,3,1,0:T(8,128)S(1)}, u32[]{:S(2)}, u32[]{:S(2)}) collective-permute-start(f32[2,2,128,256]{2,3,1,0:T(8,128)S(1)} %get-tuple-element.1355), channel_id=1, source_target_pairs={{16,0},{32,16},{48,32},{64,48},{80,64},{96,80},{112,96},{17,1},{33... | collective-permute-start | bytes 1572872 | tf_op jit(solution)/shard_map/ppermute | solution.py:26
  25.1 15.2 %copy-start.13 = (f32[2,2,128,256]{2,3,1,0:T(8,128)}, f32[2,2,128,256]{2,3,1,0:T(8,128)S(1)}, u32[]{:S(2)}) copy-start(f32[2,2,128,256]{2,3,1,0:T(8,128)S(1)} %collective-permute-done) | copy-start | bytes 1572868
  38.5 1.8 copy-start.15
  40.3 11.2 %copy-start.18 = (s32[2,1,1]{0,2,1:T(1,128)S(1)}, s32[2,1,1]{0,2,1:T(1,128)}, u32[]{:S(2)}) copy-start(s32[2,1,1]{0,2,1:T(1,128)} %param.29) | copy-start | bytes 28
  40.3 11.9 %copy-start.17 = (s32[2,2,3,1]{2,3,1,0:T(1,128)S(1)}, s32[2,2,3,1]{2,3,1,0:T(1,128)}, u32[]{:S(2)}) copy-start(s32[2,2,3,1]{2,3,1,0:T(1,128)} %param.28) | copy-start | bytes 148
  40.3 16.7 %collective-permute-start.2 = (f32[2,2,512,128]{2,3,1,0:T(8,128)}, f32[2,2,512,128]{2,3,1,0:T(8,128)}, u32[]{:S(2)}, u32[]{:S(2)}) collective-permute-start(f32[2,2,512,128]{2,3,1,0:T(8,128)} %get-tuple-element.1348), channel_id=1, source_target_pairs={{0,1},{1,2},{2,3},{3,4},{4,5},{5,6},{6,7},{7,8},{8,9},{9,10},{10,1... | collective-permute-start | bytes 3145736 | tf_op jit(solution)/shard_map/ppermute | solution.py:25
  45.0 16.4 %collective-permute-start.3 = (f32[2,2,512,128]{2,3,1,0:T(8,128)}, f32[2,2,512,128]{2,3,1,0:T(8,128)}, u32[]{:S(2)}, u32[]{:S(2)}) collective-permute-start(f32[2,2,512,128]{2,3,1,0:T(8,128)} %get-tuple-element.1349), channel_id=1, source_target_pairs={{1,0},{2,1},{3,2},{4,3},{5,4},{6,5},{7,6},{8,7},{9,8},{10,9},{11,1... | collective-permute-start | bytes 3145736 | tf_op jit(solution)/shard_map/ppermute | solution.py:26
  47.3 14.1 %copy-start.14 = (f32[2,2,128,256]{2,3,1,0:T(8,128)S(1)}, f32[2,2,128,256]{2,3,1,0:T(8,128)}, u32[]{:S(2)}) copy-start(f32[2,2,128,256]{2,3,1,0:T(8,128)} %copy-done.13) | copy-start | bytes 1572868
  68.6 37.8 %copy-start.6 = (f32[3,256,256]{1,2,0:T(8,128)}, f32[3,256,256]{1,2,0:T(8,128)S(1)}, u32[]{:S(2)}) copy-start(f32[3,256,256]{1,2,0:T(8,128)S(1)} %get-tuple-element.1627) | copy-start | bytes 2359300 | tf_op jit(solution)/shard_map/while
  144.2 13.6 %copy-start.7 = (f32[3,256,256]{1,2,0:T(8,128)S(1)}, f32[3,256,256]{1,2,0:T(8,128)}, u32[]{:S(2)}) copy-start(f32[3,256,256]{1,2,0:T(8,128)} %copy-done.6) | copy-start | bytes 2359300 | tf_op jit(solution)/shard_map/while
  158.0 38.0 %copy-start.6 = (f32[3,256,256]{1,2,0:T(8,128)}, f32[3,256,256]{1,2,0:T(8,128)S(1)}, u32[]{:S(2)}) copy-start(f32[3,256,256]{1,2,0:T(8,128)S(1)} %get-tuple-element.1627) | copy-start | bytes 2359300 | tf_op jit(solution)/shard_map/while
  234.1 13.3 %copy-start.7 = (f32[3,256,256]{1,2,0:T(8,128)S(1)}, f32[3,256,256]{1,2,0:T(8,128)}, u32[]{:S(2)}) copy-start(f32[3,256,256]{1,2,0:T(8,128)} %copy-done.6) | copy-start | bytes 2359300 | tf_op jit(solution)/shard_map/while
  247.6 38.1 %copy-start.6 = (f32[3,256,256]{1,2,0:T(8,128)}, f32[3,256,256]{1,2,0:T(8,128)S(1)}, u32[]{:S(2)}) copy-start(f32[3,256,256]{1,2,0:T(8,128)S(1)} %get-tuple-element.1627) | copy-start | bytes 2359300 | tf_op jit(solution)/shard_map/while
  323.6 13.6 %copy-start.7 = (f32[3,256,256]{1,2,0:T(8,128)S(1)}, f32[3,256,256]{1,2,0:T(8,128)}, u32[]{:S(2)}) copy-start(f32[3,256,256]{1,2,0:T(8,128)} %copy-done.6) | copy-start | bytes 2359300 | tf_op jit(solution)/shard_map/while
  340.7 6.4 copy-start
  342.5 13.8 %collective-permute-start.4 = (f32[2,2,512,128]{3,2,1,0:T(8,128)S(1)}, f32[2,2,512,128]{3,2,1,0:T(8,128)S(1)}, u32[]{:S(2)}, u32[]{:S(2)}) collective-permute-start(f32[2,2,512,128]{3,2,1,0:T(8,128)S(1)} %get-tuple-element.1341), channel_id=1, source_target_pairs={{0,1},{1,2},{2,3},{3,4},{4,5},{5,6},{6,7},{7,8},{8,9},{9,10},{10,1... | collective-permute-start | bytes 3145736 | tf_op jit(solution)/shard_map/ppermute | solution.py:15
  344.6 16.1 %collective-permute-start.5 = (f32[2,2,512,128]{3,2,1,0:T(8,128)S(1)}, f32[2,2,512,128]{3,2,1,0:T(8,128)S(1)}, u32[]{:S(2)}, u32[]{:S(2)}) collective-permute-start(f32[2,2,512,128]{3,2,1,0:T(8,128)S(1)} %get-tuple-element.1340), channel_id=1, source_target_pairs={{1,0},{2,1},{3,2},{4,3},{5,4},{6,5},{7,6},{8,7},{9,8},{10,9},{11,1... | collective-permute-start | bytes 3145736 | tf_op jit(solution)/shard_map/ppermute | solution.py:15
  360.9 25.3 %copy-start.8 = (f32[2,2,256,256]{3,2,1,0:T(8,128)S(1)}, f32[2,2,256,256]{3,2,1,0:T(8,128)}, u32[]{:S(2)}) copy-start(f32[2,2,256,256]{3,2,1,0:T(8,128)} %param.25) | copy-start | bytes 3145732
  361.0 11.7 %collective-permute-start.6 = (f32[2,2,128,256]{3,2,1,0:T(8,128)S(1)}, f32[2,2,128,256]{3,2,1,0:T(8,128)S(1)}, u32[]{:S(2)}, u32[]{:S(2)}) collective-permute-start(f32[2,2,128,256]{3,2,1,0:T(8,128)S(1)} %get-tuple-element.1347), channel_id=1, source_target_pairs={{0,16},{16,32},{32,48},{48,64},{64,80},{80,96},{96,112},{1,17},{17... | collective-permute-start | bytes 1572872 | tf_op jit(solution)/shard_map/ppermute | solution.py:15
  366.6 19.4 %collective-permute-start.7 = (f32[2,2,128,256]{3,2,1,0:T(8,128)S(1)}, f32[2,2,128,256]{3,2,1,0:T(8,128)S(1)}, u32[]{:S(2)}, u32[]{:S(2)}) collective-permute-start(f32[2,2,128,256]{3,2,1,0:T(8,128)S(1)} %get-tuple-element.1346), channel_id=1, source_target_pairs={{16,0},{32,16},{48,32},{64,48},{80,64},{96,80},{112,96},{17,1},{33... | collective-permute-start | bytes 1572872 | tf_op jit(solution)/shard_map/ppermute | solution.py:15
  386.4 55.2 %copy-start.3 = (f32[2,2,256,256]{3,2,1,0:T(8,128)}, f32[2,2,256,256]{3,2,1,0:T(8,128)S(1)}, u32[]{:S(2)}) copy-start(f32[2,2,256,256]{3,2,1,0:T(8,128)S(1)} %multiply_subtract_fusion.2) | copy-start | bytes 3145732
  386.5 12.5 %collective-permute-start.8 = (f32[2,2,128,256]{3,2,1,0:T(8,128)S(1)}, f32[2,2,128,256]{3,2,1,0:T(8,128)S(1)}, u32[]{:S(2)}, u32[]{:S(2)}) collective-permute-start(f32[2,2,128,256]{3,2,1,0:T(8,128)S(1)} %get-tuple-element.1352), channel_id=1, source_target_pairs={{0,16},{16,32},{32,48},{48,64},{64,80},{80,96},{96,112},{1,17},{17... | collective-permute-start | bytes 1572872 | tf_op jit(solution)/shard_map/ppermute | solution.py:25
  391.1 35.9 %copy-start.12 = (f32[1,3,1,256,256]{4,3,2,1,0:T(8,128)S(1)}, f32[1,3,1,256,256]{4,3,2,1,0:T(8,128)}, u32[]{:S(2)}) copy-start(f32[1,3,1,256,256]{4,3,2,1,0:T(8,128)} %get-tuple-element.1350) | copy-start | bytes 2359300
  391.2 22.4 %collective-permute-start.9 = (f32[2,2,128,256]{3,2,1,0:T(8,128)S(1)}, f32[2,2,128,256]{3,2,1,0:T(8,128)S(1)}, u32[]{:S(2)}, u32[]{:S(2)}) collective-permute-start(f32[2,2,128,256]{3,2,1,0:T(8,128)S(1)} %get-tuple-element.1353), channel_id=1, source_target_pairs={{16,0},{32,16},{48,32},{64,48},{80,64},{96,80},{112,96},{17,1},{33... | collective-permute-start | bytes 1572872 | tf_op jit(solution)/shard_map/ppermute | solution.py:26
  413.6 1.7 copy-start.16
  415.3 21.9 %collective-permute-start.10 = (f32[2,2,512,128]{3,2,1,0:T(8,128)}, f32[2,2,512,128]{3,2,1,0:T(8,128)}, u32[]{:S(2)}, u32[]{:S(2)}) collective-permute-start(f32[2,2,512,128]{3,2,1,0:T(8,128)} %get-tuple-element.1344), channel_id=1, source_target_pairs={{0,1},{1,2},{2,3},{3,4},{4,5},{5,6},{6,7},{7,8},{8,9},{9,10},{10,1... | collective-permute-start | bytes 3145736 | tf_op jit(solution)/shard_map/ppermute | solution.py:25
  425.1 16.4 %collective-permute-start.11 = (f32[2,2,512,128]{3,2,1,0:T(8,128)}, f32[2,2,512,128]{3,2,1,0:T(8,128)}, u32[]{:S(2)}, u32[]{:S(2)}) collective-permute-start(f32[2,2,512,128]{3,2,1,0:T(8,128)} %get-tuple-element.1345), channel_id=1, source_target_pairs={{1,0},{2,1},{3,2},{4,3},{5,4},{6,5},{7,6},{8,7},{9,8},{10,9},{11,1... | collective-permute-start | bytes 3145736 | tf_op jit(solution)/shard_map/ppermute | solution.py:26
  445.7 2.6 copy-start.19
  445.7 2.6 copy-start.20
  723.8 8.6 copy-start.1
  726.9 9.9 %copy-start.2 = (f32[2,2,256,256]{2,3,1,0:T(8,128)S(1)}, f32[2,2,256,256]{2,3,1,0:T(8,128)}, u32[]{:S(2)}) copy-start(f32[2,2,256,256]{2,3,1,0:T(8,128)} %get-tuple-element.843) | copy-start | bytes 3145732
  726.9 14.1 %collective-permute-start.12 = (f32[2,2,512,128]{3,2,1,0:T(8,128)}, f32[2,2,512,128]{3,2,1,0:T(8,128)}, u32[]{:S(2)}, u32[]{:S(2)}) collective-permute-start(f32[2,2,512,128]{3,2,1,0:T(8,128)} %get-tuple-element.1339), channel_id=1, source_target_pairs={{0,1},{1,2},{2,3},{3,4},{4,5},{5,6},{6,7},{7,8},{8,9},{9,10},{10,1... | collective-permute-start | bytes 3145736 | tf_op jit(solution)/shard_map/ppermute | solution.py:15
  729.0 16.4 %collective-permute-start.13 = (f32[2,2,512,128]{3,2,1,0:T(8,128)}, f32[2,2,512,128]{3,2,1,0:T(8,128)}, u32[]{:S(2)}, u32[]{:S(2)}) collective-permute-start(f32[2,2,512,128]{3,2,1,0:T(8,128)} %get-tuple-element.1338), channel_id=1, source_target_pairs={{1,0},{2,1},{3,2},{4,3},{5,4},{6,5},{7,6},{8,7},{9,8},{10,9},{11,1... | collective-permute-start | bytes 3145736 | tf_op jit(solution)/shard_map/ppermute | solution.py:15
  733.7 4.5 copy-start.11
  738.2 2.9 copy-start.5
  740.7 215.7 %all-reduce.3.cloned.1.call-start = ((), (), s32[]{:S(2)}) async-start(), calls=%async_computation | async-start | bytes 2097152 | tf_op jit(solution)/shard_map/psum | solution.py:191
  746.9 87.6 %copy-start.4 = (f32[2,2,256,256]{3,2,1,0:T(8,128)S(1)}, f32[2,2,256,256]{3,2,1,0:T(8,128)}, u32[]{:S(2)}) copy-start(f32[2,2,256,256]{3,2,1,0:T(8,128)} %copy-done.3) | copy-start | bytes 3145732
  748.0 84.1 %collective-permute-start.14 = (f32[2,2,128,256]{3,2,1,0:T(8,128)}, f32[2,2,128,256]{3,2,1,0:T(8,128)}, u32[]{:S(2)}, u32[]{:S(2)}) collective-permute-start(f32[2,2,128,256]{3,2,1,0:T(8,128)} %get-tuple-element.1343), channel_id=1, source_target_pairs={{0,16},{16,32},{32,48},{48,64},{64,80},{80,96},{96,112},{1,17},{17... | collective-permute-start | bytes 1572872 | tf_op jit(solution)/shard_map/ppermute | solution.py:15
  754.2 79.1 %collective-permute-start.15 = (f32[2,2,128,256]{3,2,1,0:T(8,128)}, f32[2,2,128,256]{3,2,1,0:T(8,128)}, u32[]{:S(2)}, u32[]{:S(2)}) collective-permute-start(f32[2,2,128,256]{3,2,1,0:T(8,128)} %get-tuple-element.1342), channel_id=1, source_target_pairs={{16,0},{32,16},{48,32},{64,48},{80,64},{96,80},{112,96},{17,1},{33... | collective-permute-start | bytes 1572872 | tf_op jit(solution)/shard_map/ppermute | solution.py:15
  833.3 123.1 %copy-start.10 = (f32[2,2,256,256]{3,2,1,0:T(8,128)S(1)}, f32[2,2,256,256]{3,2,1,0:T(8,128)}, u32[]{:S(2)}) copy-start(f32[2,2,256,256]{3,2,1,0:T(8,128)} %param.26) | copy-start | bytes 3145732
Sparse Core Ops, SparseCore 0:
  740.8 91.2 all-reduce.4
  834.5 121.8 all-reduce.2
